TPU v7x, 256 devices: a whole 4x4x8 slice. The times are simulated.
256 devices in a mesh: tile: 64 (over z, x, core), hour: 4 (over y).
Axes of the slice: x: 4, y: 4, z: 8, core: 2. Of those that a mesh axis runs over, the one named last changes fastest.
Arguments:
- spectra: float32 [32, 6, 1024, 512], P('hour', None, 'tile'), may hold values from -170 to 170
- send_list: int32 [64, 64, 2], P('tile'), may hold values from 0 to 16, as said below
- pair_list: int32 [64, 64, 2], P('tile'), may hold values from 0 to 127, as said below
- pair_count: int32 [64], P('tile'), may hold values from 1 to 64, as said below
Outputs:
- correlations: float32 [4096, 9216], P(('tile', 'hour'))
Inputs may be any that keep to these rules, and one draw needn't show every extreme that they name: `send_list`: entries [o, t, :] name different stations of owner o's block; between 1 and 2 are used and come first, unused ones hold 16. Every owner fills its 2 slots for some tile, and one tile gets 2 stations from every owner. `pair_list`: slot o * 2 + j of tile t's pool holds the j-th station that owner o sends to t; each pair names two different used slots of its tile's pool. Only pairs p < pair_count[t] of tile t are live; some tile has all 64.
All inputs are finite; a program needn't handle non-finite values.
Results may differ from a plain program's by a relative error of at most 0.0003.
Values sent between devices are 32-bit elements; how exact they have to be, the bound alone decides.
A program may use at most 128 MiB of HBM per device.

v0:
```python
import math

import jax
import jax.numpy as jnp
from jax import lax
from jax.sharding import PartitionSpec as P

NFFT = 2048
LAGS = 1024


def whiten(spectra):
    real_part = spectra[:, 0::2]
    imag_part = spectra[:, 1::2]
    power_sum = jnp.sum(real_part * real_part + imag_part * imag_part, axis=1)
    bin_count = power_sum.shape[-1]
    padded = jnp.pad(power_sum, ((0, 0), (0, 0), (2, 2)))
    smoothed = (
        padded[..., 0:bin_count]
        + padded[..., 1 : bin_count + 1]
        + padded[..., 2 : bin_count + 2]
        + padded[..., 3 : bin_count + 3]
        + padded[..., 4 : bin_count + 4]
    ) / 15.0
    water_level = jnp.sum(power_sum, axis=-1, keepdims=True) / (3.0 * bin_count)
    return spectra / jnp.sqrt(smoothed + 0.25 * water_level + 1e-06)[:, None]


def pair_sums(pooled, first_slot, second_slot):
    first_rows = jnp.take(pooled, first_slot, axis=2)
    second_rows = jnp.take(pooled, second_slot, axis=2)
    results = []
    for first_comp in range(3):
        first_real = first_rows[:, 2 * first_comp]
        first_imag = first_rows[:, 2 * first_comp + 1]
        for second_comp in range(3):
            second_real = second_rows[:, 2 * second_comp]
            second_imag = second_rows[:, 2 * second_comp + 1]
            real_sum = jnp.sum(first_real * second_real + first_imag * second_imag, axis=0)
            imag_sum = jnp.sum(first_imag * second_real - first_real * second_imag, axis=0)
            results.append(jnp.stack([real_sum, imag_sum]))
    return jnp.stack(results)


def lag_table(bin_count, lag_count, length, segment_total):
    frequency = jnp.arange(bin_count, dtype=jnp.int32)
    lag_index = jnp.arange(lag_count, dtype=jnp.int32) - lag_count // 2
    phases = jnp.mod(frequency[:, None] * lag_index[None, :], length).astype(jnp.float32) * (
        2.0 * math.pi / length
    )
    normalizer = 1.0 / math.sqrt(bin_count * segment_total)
    return jnp.stack([jnp.cos(phases) * normalizer, -jnp.sin(phases) * normalizer])


def body(spectra, send_list, pair_list, pair_count):
    segment_count = spectra.shape[0]
    block_size = spectra.shape[2]
    bin_count = spectra.shape[3]
    hour_count = lax.axis_size("hour")
    whitened = whiten(spectra)
    picked = send_list[0]
    used_mask = picked < block_size
    chosen = jnp.where(used_mask, picked, 0).reshape(-1)
    used_scale = used_mask.reshape(-1).astype(jnp.float32)[:, None]
    pair_rows = pair_list[0]
    first_slot = pair_rows[:, 0]
    second_slot = pair_rows[:, 1]
    slot_count = pair_rows.shape[0]
    selected = jnp.take(whitened, chosen, axis=2) * used_scale
    received = lax.all_to_all(selected, "tile", split_axis=2, concat_axis=2, tiled=True)
    spectral_sum = pair_sums(received, first_slot, second_slot)
    live_mask = (jnp.arange(slot_count, dtype=jnp.int32) < pair_count[0]).astype(jnp.float32)
    spectral_sum = spectral_sum * live_mask[:, None]
    weights_table = lag_table(bin_count, LAGS, NFFT, segment_count * hour_count)
    own_rows = slot_count // hour_count
    summed = lax.psum_scatter(spectral_sum, "hour", scatter_dimension=2, tiled=True)
    lagged = jnp.einsum("csqf,sfl->qcl", summed, weights_table, precision=lax.Precision.HIGHEST)
    return lagged.reshape(own_rows, 9 * LAGS)


def solution(mesh):
    in_specs = (
        P("hour", None, "tile", None),
        P("tile", None, None),
        P("tile", None, None),
        P("tile"),
    )
    out_specs = P(("tile", "hour"), None)
    return jax.shard_map(body, mesh=mesh, in_specs=in_specs, out_specs=out_specs, check_vma=False)
```

profile of v0, /device:TPU:1, one launch (start us, length us, event | category | flops | bytes accessed | tf_op | source)
XLA Modules:
  0.0 409.6 jit_solution(14722444070092265179)
XLA Ops:
  6.5 0.0 copy-start.1
  6.5 0.9 copy.13
  7.4 0.1 squeeze.13
  7.6 0.1 squeeze.12
  7.7 1.6 fusion.27
  9.3 0.4 fusion.17
  9.7 0.2 copy.14
  9.9 0.0 copy-done.1
  9.9 0.9 copy_divide_fusion
  10.9 5.9 %gather_fusion = f32[128,8,6,512]{3,1,2,0:T(8,128)} fusion(f32[8,6,16,512]{3,0,2,1:T(8,128)S(1)} %copy_divide_fusion, s32[1024]{0:T(1024)S(1)} %pad_clamp_fusion.2), kind=kCustom, calls=%fused_computation.2 | custom fusion | bytes 25166336 | tf_op jit(solution)/shard_map/jit(_take)/gather | solution.py:69
  16.8 12.1 %multiply_bitcast_fusion = f32[8,6,128,512]{3,0,1,2:T(8,128)} fusion(f32[128,8,6,512]{3,1,2,0:T(8,128)} %gather_fusion, f32[128]{0:T(128)S(1)} %get-tuple-element.43, pred[128]{0:T(512)(128)(4,1)S(1)} %get-tuple-element.42), kind=kLoop, calls=%fused_computation.3 | loop fusion | flops 6291456 | bytes 25166464 | tf_op jit(solution)/shard_map/mul | solution.py:69
  28.9 0.0 copy-start.2
  28.9 13.3 %all-to-all-start = ((f32[8,6,128,512]{3,0,1,2:T(8,128)}), f32[8,6,128,512]{3,0,1,2:T(8,128)}, u32[]{:S(2)}, u32[]{:S(2)}) async-start(f32[8,6,128,512]{3,0,1,2:T(8,128)} %multiply_bitcast_fusion), calls=%async_computation | async-start | bytes 25165824 | tf_op jit(solution)/shard_map/all_to_all | solution.py:70
  42.2 0.2 reduce-scatter.2.cloned.1.call-start
  43.1 0.0 copy-done.2
  43.1 271.2 %all-to-all-done = f32[8,6,128,512]{3,0,1,2:T(8,128)} async-done(((f32[8,6,128,512]{3,0,1,2:T(8,128)}), f32[8,6,128,512]{3,0,1,2:T(8,128)}, u32[]{:S(2)}, u32[]{:S(2)}) %all-to-all-start) | async-done | bytes 12582944 | tf_op jit(solution)/shard_map/all_to_all | solution.py:70
  314.3 11.3 %copy.17 = f32[8,6,128,512]{3,0,2,1:T(8,128)} copy(f32[8,6,128,512]{3,0,1,2:T(8,128)} %all-to-all-done) | data formatting | bytes 25165824 | tf_op jit(solution)/shard_map/all_to_all | solution.py:70
  325.6 8.1 %gather_fusion.1 = f32[64,8,6,512]{3,1,2,0:T(8,128)} fusion(f32[8,6,128,512]{3,0,2,1:T(8,128)} %copy.17, s32[1024]{0:T(1024)S(1)} %get-tuple-element.45), kind=kCustom, calls=%fused_computation.clone | custom fusion | bytes 12583168 | tf_op jit(solution)/shard_map/jit(_take)/gather | solution.py:30
  333.7 8.1 %gather_fusion.2 = f32[64,8,6,512]{3,1,2,0:T(8,128)} fusion(f32[8,6,128,512]{3,0,2,1:T(8,128)} %copy.17, s32[1024]{0:T(1024)S(1)} %get-tuple-element.44), kind=kCustom, calls=%fused_computation.1.clone | custom fusion | bytes 12583168 | tf_op jit(solution)/shard_map/jit(_take)/gather | solution.py:31
  341.8 0.0 copy-start
  341.8 4.0 select_bitcast_fusion.1
  345.8 0.6 copy-done
  346.4 1.3 select_bitcast_fusion
  347.8 1.0 add_reduce_fusion.8
  348.8 3.3 add_reduce_fusion.1
  352.0 4.0 add_reduce_fusion.2
  356.3 1.8 broadcast_multiply_fusion
  358.1 0.0 reduce-scatter.2.cloned.1.call-update
  358.1 9.3 %cosine_multiply_fusion = (f32[1,512,1024]{2,1,0:T(8,128)S(1)}, f32[1,512,1024]{2,1,0:T(8,128)}) fusion(s32[1024]{0:T(1024)S(1)} %iota_add_fusion), kind=kLoop, calls=%fused_computation.17 | loop fusion | flops 8912896 | bytes 4198400 | tf_op jit(solution)/shard_map/mul | solution.py:52
  367.4 30.2 %reduce-scatter.2.cloned.1.call-done = f32[9,2,16,512]{3,2,1,0:T(8,128)} async-done(((f32[9,2,64,512]{3,2,1,0:T(8,128)}), f32[9,2,16,512]{3,2,1,0:T(8,128)}) %reduce-scatter.2.cloned.1.call-update) | async-done | bytes 589840 | tf_op jit(solution)/shard_map/reduce_scatter | solution.py:76
  397.6 4.3 %fusion.9 = f32[9,2,8,1024]{3,2,1,0:T(8,128)S(1)} fusion(f32[9,2,16,512]{3,2,1,0:T(8,128)} %reduce-scatter.2.cloned.1.call-done, f32[1,512,1024]{2,1,0:T(8,128)} %get-tuple-element.39, f32[1,512,1024]{2,1,0:T(8,128)S(1)} %get-tuple-element.38), kind=kOutput, calls=%fused_computation.22 | convolution fusion | flops 1812987904 | bytes 5373952 | tf_op jit(solution)/shard_map/csqf,sfl->qcl/dot_general | solution.py:77
  401.9 0.9 copy.21
  (17 shorter events, 0.2 us)
Async XLA Ops:
  6.5 3.3 copy-start.1
  28.9 14.2 %copy-start.2 = (s32[1,64,2]{1,2,0:T(2,128)S(1)}, s32[1,64,2]{1,2,0:T(2,128)}, u32[]{:S(2)}) copy-start(s32[1,64,2]{1,2,0:T(2,128)} %param.8) | copy-start | bytes 1540
  28.9 285.4 %all-to-all-start = ((f32[8,6,128,512]{3,0,1,2:T(8,128)}), f32[8,6,128,512]{3,0,1,2:T(8,128)}, u32[]{:S(2)}, u32[]{:S(2)}) async-start(f32[8,6,128,512]{3,0,1,2:T(8,128)} %multiply_bitcast_fusion), calls=%async_computation | async-start | bytes 25165824 | tf_op jit(solution)/shard_map/all_to_all | solution.py:70
  42.2 355.4 %reduce-scatter.2.cloned.1.call-start = ((), (), s32[]{:S(2)}) async-start(), calls=%async_computation.2 | async-start | bytes 2949120 | tf_op jit(solution)/shard_map/reduce_scatter | solution.py:76
  341.8 4.6 %copy-start = (f32[64,8,6,512]{3,1,2,0:T(8,128)S(1)}, f32[64,8,6,512]{3,1,2,0:T(8,128)}, u32[]{:S(2)}) copy-start(f32[64,8,6,512]{3,1,2,0:T(8,128)} %gather_fusion.2) | copy-start | bytes 18874372
Sparse Core Ops, SparseCore 0:
  358.2 39.3 reduce-scatter.1
where the time goes:
time: 410 us
  waiting for transfers between devices  301 us (73%)
  other arithmetic  39.8 us (10%)
  local copies, waits for them, and re-layouts  36.3 us (9%)
  between operations  14.3 us (3%)
  starting transfers between devices  13.5 us (3%)
  matrix products  4.27 us (1%)
    all_to_all x1, waiting for transfers between devices, body(): lax.all_to_all(selected, 'tile', split_axis=2, concat_axis=2, tiled=True)  271 us
    reduce_scatter x1, waiting for transfers between devices, body(): lax.psum_scatter(spectral_sum, 'hour', scatter_dimension=2, tiled=True)  30.2 us
    all_to_all x1, starting transfers between devices, body(): lax.all_to_all(selected, 'tile', split_axis=2, concat_axis=2, tiled=True)  13.3 us
    mul x1, other arithmetic, body(): selected = jnp.take(whitened, chosen, axis=2) * used_scale  12.1 us
    all_to_all x1, local copies, waits for them, and re-layouts, body(): lax.all_to_all(selected, 'tile', split_axis=2, concat_axis=2, tiled=True)  11.3 us
    mul x1, other arithmetic, lag_table(): jnp.cos(phases) * normalizer  9.27 us
    reduce_sum x3, other arithmetic, pair_sums(): jnp.sum(first_real * second_real + first_imag * second_imag, axis=0)  8.25 us
  transfers between devices with their start and end apart: 2, of which 2 were waited for; matrix products, arithmetic and copies ran while one was open for 2% of the time, Pallas kernels for 0%

commit v1 on v0

v1 whole, which is shorter than its diff:
```python
import functools
import math

import jax
import jax.numpy as jnp
from jax import lax
from jax.experimental import pallas as pl
from jax.experimental.pallas import tpu as pltpu
from jax.sharding import PartitionSpec as P

MESH = pl.DeviceIdType.MESH
F32, BF16, I32 = jnp.float32, jnp.bfloat16, jnp.int32

NFFT = 2048
LAGS = 1024
BINS = 512
SEGS = 32
HS = 8
STB = 16
NT, NH = 64, 4
ND = NT * NH
CH = 12
RR = 5


def position():
    t = lax.axis_index("tile")
    return t, lax.axis_index("hour"), t // 8, t % 8


def entry_barrier(signal_only=False):
    t, h, z, xc = position()
    bar = pltpu.get_barrier_semaphore()
    for i in range(1, 8):
        pl.semaphore_signal(bar, inc=1, device_id=(((z + i) % 8) * 8 + xc, h), device_id_type=MESH)
    for i in range(1, 8):
        pl.semaphore_signal(bar, inc=1, device_id=(z * 8 + (xc + i) % 8, h), device_id_type=MESH)
    for i in range(1, NH):
        pl.semaphore_signal(bar, inc=1, device_id=(t, (h + i) % NH), device_id_type=MESH)


def entry_barrier_rest(plane_sem, all_sem):
    t, h, z, xc = position()
    pl.semaphore_wait(pltpu.get_barrier_semaphore(), 17)
    for i in range(1, 8):
        pl.semaphore_signal(plane_sem, inc=1, device_id=(z * 8 + (xc + i) % 8, h), device_id_type=MESH)
    pl.semaphore_wait(plane_sem, 7)
    for i in range(1, NH):
        pl.semaphore_signal(all_sem, inc=1, device_id=(t, (h + i) % NH), device_id_type=MESH)
    pl.semaphore_wait(all_sem, NH - 1)


def peer(i):
    t, h, z, xc = position()
    x, c = xc // 2, xc % 2
    z2 = (z + (i // 2) % 8) % 8
    x2 = (x + (i // 16) % 4) % 4
    c2 = (c + i) % 2
    return (z2 * 4 + x2) * 2 + c2, (h + i // 64) % NH


def roll(x, shift, axis):
    return pltpu.roll(x, shift, axis)


def swap_blocks(x):
    sub = lax.broadcasted_iota(I32, (8, 128), 0)
    lane = lax.broadcasted_iota(I32, (8, 128), 1)
    for b in (1, 2, 4):
        step = 16 * b
        sb = (sub & b) != 0
        lb = (lane & step) != 0
        down = roll(roll(x, 8 - b, 0), step, 1)
        up = roll(roll(x, b, 0), 128 - step, 1)
        x = jnp.where(sb == lb, x, jnp.where(sb, up, down))
    return x


def spread_kernel(spec_ref, lists_ref, recv_ref, lout_ref, white, pack, plane_sem, all_sem, send_sem, recv_sem,
                  lsend_sem, lrecv_sem, loc_sem, lloc_sem):
    t, h, _, _ = position()
    entry_barrier()
    lane = lax.broadcasted_iota(I32, (STB, BINS), 1)

    def whiten(s, carry):
        x = spec_ref[s]
        power = jnp.sum(x * x, axis=0)
        total = power
        total += jnp.where(lane >= 1, roll(power, 1, 1), 0.0)
        total += jnp.where(lane >= 2, roll(power, 2, 1), 0.0)
        total += jnp.where(lane < BINS - 1, roll(power, BINS - 1, 1), 0.0)
        total += jnp.where(lane < BINS - 2, roll(power, BINS - 2, 1), 0.0)
        water = jnp.sum(power, axis=1, keepdims=True) * (1.0 / (3.0 * BINS))
        inv = 1.0 / jnp.sqrt(total * (1.0 / 15.0) + 0.25 * water + 1e-06)
        white[:, pl.ds(pl.multiple_of(s * STB, STB), STB), :] = x * inv[None]
        return carry

    lax.fori_loop(0, HS, whiten, 0)
    for c in range(6):
        for kb in range(4):
            block = white[c, :, kb * 128:(kb + 1) * 128].T
            pack[pl.ds((kb % 2) * 128, 128), (kb // 2) * 6 + c, :] = block
    entry_barrier_rest(plane_sem, all_sem)
    me = t * NH + h
    own = pltpu.make_async_copy(pack.at[h * NT + t], recv_ref.at[me], loc_sem)
    own.start()
    lown = pltpu.make_async_copy(lists_ref, lout_ref.at[t], lloc_sem)
    lown.start()

    def send_lists(i, carry):
        t2, _ = peer(i)
        pltpu.make_async_remote_copy(src_ref=lists_ref, dst_ref=lout_ref.at[t], send_sem=lsend_sem,
                                     recv_sem=lrecv_sem, device_id=(t2, h), device_id_type=MESH).start()
        return carry

    def send(i, carry):
        t2, h2 = peer(i)
        pltpu.make_async_remote_copy(src_ref=pack.at[h2 * NT + t2], dst_ref=recv_ref.at[me], send_sem=send_sem,
                                     recv_sem=recv_sem, device_id=(t2, h2), device_id_type=MESH).start()
        return carry

    lax.fori_loop(1, ND, send, 0)
    lax.fori_loop(1, NT, send_lists, 0)
    own.wait()
    lown.wait()
    rest, lrest = pl.ds(0, ND - 1), pl.ds(0, NT - 1)
    pltpu.make_async_copy(pack.at[rest], pack.at[rest], send_sem).wait()
    pltpu.make_async_copy(recv_ref.at[rest], recv_ref.at[rest], recv_sem).wait()
    pltpu.make_async_copy(lout_ref.at[lrest], lout_ref.at[lrest], lsend_sem).wait()
    pltpu.make_async_copy(lout_ref.at[lrest], lout_ref.at[lrest], lrecv_sem).wait()


def spread(spectra, lists):
    vmem = pl.BlockSpec(memory_space=pltpu.VMEM)
    sem = pltpu.SemaphoreType
    return pl.pallas_call(
        spread_kernel,
        out_shape=(jax.ShapeDtypeStruct((ND, CH, 128), F32), jax.ShapeDtypeStruct((NT, 2, 128), I32)),
        in_specs=[vmem, vmem],
        out_specs=(vmem, vmem),
        scratch_shapes=[pltpu.VMEM((6, HS * STB, BINS), F32), pltpu.VMEM((ND, CH, 128), F32),
                        sem.REGULAR, sem.REGULAR] + [sem.DMA] * 6,
        compiler_params=pltpu.CompilerParams(collective_id=0, has_side_effects=True),
        name="spread",
    )(spectra, lists)


def resolve_stations(lout_ref, slots_ref, idx_ref):
    sends = lout_ref[:, 0, :].astype(F32)
    slots_ref[...] = jnp.concatenate([sends, jnp.zeros((64, 128), F32)], axis=0).T
    first = slots_ref[pl.ds(0, NT, stride=2), :]
    second = slots_ref[pl.ds(1, NT, stride=2), :]
    slot = lout_ref[:, 1, :]
    owner = jnp.maximum(slot, 0) // 2
    pick = jnp.where(slot % 2 == 0, jnp.take_along_axis(first, owner, axis=1),
                     jnp.take_along_axis(second, owner, axis=1))
    station = owner.astype(F32) * STB + pick
    station = jnp.where((slot < 0) | (pick >= STB), -1.0, station)
    for tg in range(8):
        idx_ref[tg] = swap_blocks(station[tg * 8:(tg + 1) * 8])


def build_table(recv_ref, table_ref):
    sub = lax.broadcasted_iota(I32, (8, 128), 0)
    lane = lax.broadcasted_iota(I32, (8, 128), 1)
    l16, l32, l64 = (lane & 16) != 0, (lane & 32) != 0, (lane & 64) != 0
    same, top = ((sub & 4) != 0) == l16, (sub & 4) != 0

    def group(og, carry):
        for f in range(2):
            for ci in range(3):
                parts = []
                for c in (2 * ci, 2 * ci + 1):
                    v = []
                    for g in range(4):
                        x = recv_ref[pl.ds(og * 32 + g * 8, 8), f * 6 + c, :]
                        y = roll(x, 4, 0)
                        v.append(jnp.where(same, x, jnp.where(top, roll(y, 112, 1), roll(y, 16, 1))))
                    w = [None] * 4
                    for hi in range(2):
                        a, b = v[2 * hi], v[2 * hi + 1]
                        w[2 * hi] = jnp.where(l32, roll(b, 32, 1), a)
                        w[2 * hi + 1] = jnp.where(l32, b, roll(a, 96, 1))
                    u = [None] * 4
                    for lo in range(2):
                        a, b = w[lo], w[2 + lo]
                        u[lo] = jnp.where(l64, roll(b, 64, 1), a)
                        u[2 + lo] = jnp.where(l64, b, roll(a, 64, 1))
                    parts.append(u)
                for sv in range(4):
                    both = jnp.concatenate([parts[0][sv], parts[1][sv]], axis=0)
                    high = both.astype(BF16)
                    low = (both - high.astype(F32)).astype(BF16)
                    row = ((sv * 2 + f) * 6 + 2 * ci) * 8
                    cols = pl.ds(pl.multiple_of(og * 128, 128), 128)
                    table_ref[row:row + 16, cols] = high
                    table_ref[384 + row:384 + row + 16, cols] = low
        return carry

    lax.fori_loop(0, 8, group, 0)


def pair_kernel(recv_ref, lout_ref, out_ref, slots_ref, idx_ref, table_ref, prod_ref):
    resolve_stations(lout_ref, slots_ref, idx_ref)
    build_table(recv_ref, table_ref)
    station = lax.broadcasted_iota(I32, (1024, 256), 0)

    def block(i, carry):
        tg, h = i // NH, i % NH
        wanted = jnp.concatenate([idx_ref[tg, pl.ds(h, 1), :], idx_ref[tg, pl.ds(4 + h, 1), :]], axis=1)
        live = jnp.max(wanted) >= 0.0
        rows = pl.ds(h * NT + tg * 8, 8)

        @pl.when(live)
        def _():
            chosen = (station == wanted.astype(I32)).astype(F32).astype(BF16)
            full = jnp.dot(table_ref[...], chosen, preferred_element_type=F32)
            prod_ref[...] = full[:384] + full[384:]
            sums = {}
            for f in range(2):
                acc = [None] * 18
                for sv in range(4):
                    base = (sv * 2 + f) * 48
                    a = [prod_ref[base + 8 * c:base + 8 * c + 8, 0:128] for c in range(6)]
                    b = [prod_ref[base + 8 * c:base + 8 * c + 8, 128:256] for c in range(6)]
                    for p in range(3):
                        for q in range(3):
                            re = a[2 * p] * b[2 * q] + a[2 * p + 1] * b[2 * q + 1]
                            im = a[2 * p + 1] * b[2 * q] - a[2 * p] * b[2 * q + 1]
                            n = (p * 3 + q) * 2
                            acc[n] = re if sv == 0 else acc[n] + re
                            acc[n + 1] = im if sv == 0 else acc[n + 1] + im
                for n in range(18):
                    sums[n * 2 + f] = jnp.sum(acc[n], axis=0, keepdims=True)
            for r in range(RR):
                got = [sums.get(r * 8 + g) for g in range(8)]
                got = [jnp.zeros((1, 128), F32) if v is None else v for v in got]
                out_ref[rows, r, :] = swap_blocks(jnp.concatenate(got, axis=0))

        @pl.when(jnp.logical_not(live))
        def _():
            out_ref[rows, :, :] = jnp.zeros((8, RR, 128), F32)

        return carry

    lax.fori_loop(0, 32, block, 0)


def pair_products(received, lists):
    vmem = pl.BlockSpec(memory_space=pltpu.VMEM)
    return pl.pallas_call(
        pair_kernel,
        out_shape=jax.ShapeDtypeStruct((ND, RR, 128), F32),
        in_specs=[vmem, vmem],
        out_specs=vmem,
        scratch_shapes=[pltpu.VMEM((128, 128), F32), pltpu.VMEM((8, 8, 128), F32), pltpu.VMEM((768, 1024), BF16),
                        pltpu.VMEM((384, 256), F32)],
        name="pair_products",
    )(received, lists)


def lag_tables(high_ref, low_ref, fine_ref):
    scale = 1.0 / math.sqrt(BINS * SEGS)
    lag = lax.broadcasted_iota(I32, (32, LAGS), 1) - LAGS // 2
    fine = ((lax.broadcasted_iota(I32, (32, LAGS), 0) * lag) & (NFFT - 1)).astype(F32) * (2.0 * math.pi / NFFT)
    fine_ref[0] = jnp.cos(fine)
    fine_ref[1] = jnp.sin(fine)
    lag1 = lax.broadcasted_iota(I32, (8, LAGS), 1) - LAGS // 2

    def rows(a, carry):
        coarse = ((lag1 * (32 * a)) & (NFFT - 1)).astype(F32) * (2.0 * math.pi / NFFT)
        cosine, sine = jnp.cos(coarse)[0:1] * scale, jnp.sin(coarse)[0:1] * scale
        at = pl.multiple_of(a * 32, 32)
        for part, value in ((0, cosine * fine_ref[0] - sine * fine_ref[1]),
                            (BINS, -(sine * fine_ref[0] + cosine * fine_ref[1]))):
            high = value.astype(BF16)
            high_ref[pl.ds(part + at, 32), :] = high
            low_ref[pl.ds(part + at, 32), :] = (value - high.astype(F32)).astype(BF16)
        return carry

    lax.fori_loop(0, BINS // 32, rows, 0)


def collect_kernel(cross_ref, out_ref, recv, high_ref, low_ref, fine_ref, sum_ref, plane_sem, all_sem, send_sem,
                   recv_sem, loc_sem):
    t, h, _, _ = position()
    entry_barrier()
    me = h * NT + t
    entry_barrier_rest(plane_sem, all_sem)
    own = pltpu.make_async_copy(cross_ref.at[me], recv.at[me], loc_sem)
    own.start()

    def send(i, carry):
        t2, h2 = peer(i)
        pltpu.make_async_remote_copy(src_ref=cross_ref.at[h2 * NT + t2], dst_ref=recv.at[me], send_sem=send_sem,
                                     recv_sem=recv_sem, device_id=(t2, h2), device_id_type=MESH).start()
        return carry

    lax.fori_loop(1, ND, send, 0)
    lag_tables(high_ref, low_ref, fine_ref)
    own.wait()
    rest = pl.ds(0, ND - 1)
    pltpu.make_async_copy(cross_ref.at[rest], cross_ref.at[rest], send_sem).wait()
    pltpu.make_async_copy(recv.at[rest], recv.at[rest], recv_sem).wait()
    for r in range(RR):
        turned = recv[:, r, :].T
        for g in range(8):
            m = r * 8 + g
            if m < 36:
                sum_ref[(m // 4) * 16:(m // 4) * 16 + 16, (m % 4) * 256:(m % 4) * 256 + 256] = turned[g * 16:g * 16 + 16]
    total = sum_ref[...]
    high = total.astype(BF16)
    low = (total - high.astype(F32)).astype(BF16)
    for j in range(4):
        cols = slice(j * 256, j * 256 + 256)
        part = jnp.dot(high, high_ref[:, cols], preferred_element_type=F32)
        part += jnp.dot(high, low_ref[:, cols], preferred_element_type=F32)
        part += jnp.dot(low, high_ref[:, cols], preferred_element_type=F32)
        for c in range(9):
            out_ref[:, c * LAGS + j * 256:c * LAGS + j * 256 + 256] = part[c * 16:c * 16 + 16]


def collect(cross):
    vmem = pl.BlockSpec(memory_space=pltpu.VMEM)
    sem = pltpu.SemaphoreType
    return pl.pallas_call(
        collect_kernel,
        out_shape=jax.ShapeDtypeStruct((16, 9 * LAGS), F32),
        in_specs=[vmem],
        out_specs=vmem,
        scratch_shapes=[pltpu.VMEM((ND, RR, 128), F32), pltpu.VMEM((2 * BINS, LAGS), BF16),
                        pltpu.VMEM((2 * BINS, LAGS), BF16), pltpu.VMEM((2, 32, LAGS), F32),
                        pltpu.VMEM((144, 2 * BINS), F32), sem.REGULAR, sem.REGULAR, sem.DMA, sem.DMA, sem.DMA],
        compiler_params=pltpu.CompilerParams(collective_id=1, has_side_effects=True),
        name="collect",
    )(cross)


def body(spectra, send_list, pair_list, pair_count):
    pairs = pair_list[0]
    live = jnp.arange(pairs.shape[0], dtype=I32)[:, None] < pair_count[0]
    slots = jnp.where(live, pairs, -1).T.reshape(128)
    lists = jnp.stack([send_list[0].reshape(128), slots])
    received, all_lists = spread(spectra, lists)
    return collect(pair_products(received, all_lists))


def solution(mesh):
    in_specs = (P("hour", None, "tile", None), P("tile", None, None), P("tile", None, None), P("tile"))
    return jax.shard_map(body, mesh=mesh, in_specs=in_specs, out_specs=P(("tile", "hour"), None), check_vma=False)
```

time: 410 us -> 115 us (0.28)
  waiting for transfers between devices: 301 us -> 0 us
  Pallas kernels: 0 us -> 110 us
  other arithmetic: 39.8 us -> 1.27 us
  local copies, waits for them, and re-layouts: 36.3 us -> 2.91 us
  between operations: 14.3 us -> 0.68 us
  starting transfers between devices: 13.5 us -> 0 us
  matrix products: 4.27 us -> 0 us
    all_to_all x1 -> x0, waiting for transfers between devices: 271 us -> none  [body(): lax.all_to_all(selected, 'tile', split_axis=2, concat_axis=2, tiled=True)]
    pallas_call x0 -> x3, Pallas kernels: none -> 110 us  [the longest x1 55.2 us: spread(): pl.pallas_call(spread_kernel, out_shape=(jax.ShapeDtypeStruct((ND, CH, 12...]
    reduce_scatter x1 -> x0, waiting for transfers between devices: 30.2 us -> none  [body(): lax.psum_scatter(spectral_sum, 'hour', scatter_dimension=2, tiled=True)]
    mul x4 -> x0, other arithmetic: 23.2 us -> none  [the longest x1 12.1 us: body(): selected = jnp.take(whitened, chosen, axis=2) * used_scale]
    gather x3 -> x0, local copies, waits for them, and re-layouts: 22.2 us -> none  [the longest x1 8.13 us: pair_sums(): second_rows = jnp.take(pooled, second_slot, axis=2)]
    all_to_all x1 -> x0, starting transfers between devices: 13.3 us -> none  [body(): lax.all_to_all(selected, 'tile', split_axis=2, concat_axis=2, tiled=True)]
    all_to_all x1 -> x0, local copies, waits for them, and re-layouts: 11.3 us -> none  [body(): lax.all_to_all(selected, 'tile', split_axis=2, concat_axis=2, tiled=True)]
    reduce_sum x4 -> x0, other arithmetic: 9.84 us -> none  [the longest x3 8.25 us: pair_sums(): jnp.sum(first_real * second_real + first_imag * second_imag, axis=0)]
  transfers between devices with their start and end apart: 2 -> 0, of which waited for: 2 -> 0; matrix products, arithmetic and copies ran while one was open for 2% -> 0% of each run, Pallas kernels for 0% -> 0%
where the time goes in v1:
time: 115 us
  Pallas kernels  110 us (96%)
  local copies, waits for them, and re-layouts  2.91 us (3%)
  other arithmetic  1.27 us (1%)
    pallas_call x1, Pallas kernels, spread(): pl.pallas_call(spread_kernel, out_shape=(jax.ShapeDtypeStruct((ND, CH, 12...  55.2 us
    pallas_call x1, Pallas kernels, collect(): pl.pallas_call(collect_kernel, out_shape=jax.ShapeDtypeStruct((16, 9 * LA...  29.3 us
    pallas_call x1, Pallas kernels, pair_products(): pl.pallas_call(pair_kernel, out_shape=jax.ShapeDtypeStruct((ND, RR, 128),...  25.6 us
    unnamed x2, local copies, waits for them, and re-layouts  2.69 us

profile of v1, /device:TPU:1, one launch (start us, length us, event | category | flops | bytes accessed | tf_op | source)
XLA Modules:
  0.0 115.0 jit_solution(4413608721878243564)
XLA Ops:
  0.7 0.7 fusion
  1.4 0.1 stack_reshape.3
  1.4 0.8 copy.6
  2.2 0.1 stack_reshape_squeeze.3
  2.3 0.6 pad_add_fusion.lists_ref
  2.9 55.2 %spread.1 = (f32[256,12,128]{2,1,0:T(8,128)}, s32[64,2,128]{2,1,0:T(2,128)}) custom-call(f32[8,6,16,512]{3,2,1,0:T(8,128)} %spec_ref.1, s32[2,128]{1,0:T(2,128)} %pad_add_fusion.lists_ref), custom_call_target="tpu_custom_call" | custom-call | tf_op jit(solution)/shard_map/spread/pallas_call | solution.py:136
  58.1 25.6 %pair_products.1.cross_ref = f32[256,5,128]{2,1,0:T(8,128)} custom-call(f32[256,12,128]{2,1,0:T(8,128)} %get-tuple-element.7.recv_ref, s32[64,2,128]{2,1,0:T(2,128)} %get-tuple-element.8.lout_ref), custom_call_target="tpu_custom_call" | custom-call | tf_op jit(solution)/shard_map/pair_products/pallas_call | solution.py:251
  83.7 29.3 %collect.1 = f32[16,9216]{1,0:T(8,128)} custom-call(f32[256,5,128]{2,1,0:T(8,128)} %pair_products.1.cross_ref), custom_call_target="tpu_custom_call" | custom-call | tf_op jit(solution)/shard_map/collect/pallas_call | solution.py:326
  113.1 1.9 %copy.9 = f32[16,9216]{1,0:T(8,128)} copy(f32[16,9216]{1,0:T(8,128)} %collect.1) | data formatting | bytes 1179648
  (1 shorter events, 0.0 us)

commit v2 on v0

v2 whole, which is shorter than its diff:
```python
import functools
import math

import jax
import jax.numpy as jnp
from jax import lax
from jax.experimental import pallas as pl
from jax.experimental.pallas import tpu as pltpu
from jax.sharding import PartitionSpec as P

MESH = pl.DeviceIdType.MESH
F32, BF16, I32 = jnp.float32, jnp.bfloat16, jnp.int32

NFFT = 2048
LAGS = 1024
BINS = 512
SEGS = 32
HS = 8
STB = 16
NT, NH = 64, 4
ND = NT * NH
CH = 12
RR = 5


def position():
    t = lax.axis_index("tile")
    return t, lax.axis_index("hour"), t // 8, t % 8


def entry_barrier(signal_only=False):
    t, h, z, xc = position()
    bar = pltpu.get_barrier_semaphore()
    for i in range(1, 8):
        pl.semaphore_signal(bar, inc=1, device_id=(((z + i) % 8) * 8 + xc, h), device_id_type=MESH)
    for i in range(1, 8):
        pl.semaphore_signal(bar, inc=1, device_id=(z * 8 + (xc + i) % 8, h), device_id_type=MESH)
    for i in range(1, NH):
        pl.semaphore_signal(bar, inc=1, device_id=(t, (h + i) % NH), device_id_type=MESH)


def entry_barrier_rest(plane_sem, all_sem):
    t, h, z, xc = position()
    pl.semaphore_wait(pltpu.get_barrier_semaphore(), 17)
    for i in range(1, 8):
        pl.semaphore_signal(plane_sem, inc=1, device_id=(z * 8 + (xc + i) % 8, h), device_id_type=MESH)
    pl.semaphore_wait(plane_sem, 7)
    for i in range(1, NH):
        pl.semaphore_signal(all_sem, inc=1, device_id=(t, (h + i) % NH), device_id_type=MESH)
    pl.semaphore_wait(all_sem, NH - 1)


def each_peer(planes, act):
    t, h, z, xc = position()
    zs = [((z + d) % 8) * 8 for d in range(8)]
    cs = [(xc + d) % 2 for d in range(2)]

    def some(k, carry):
        x2, h2 = ((xc // 2 + k) % 4) * 2, (h + k // 4) % NH
        for dz in range(8):
            for dc in range(2):
                if dz + dc == 0:
                    pl.when(k > 0)(lambda: act(zs[0] + x2 + cs[0], h2))
                else:
                    act(zs[dz] + x2 + cs[dc], h2)
        return carry

    lax.fori_loop(0, 4 * planes, some, 0)


def roll(x, shift, axis):
    return pltpu.roll(x, shift, axis)


def swap_blocks(x):
    sub = lax.broadcasted_iota(I32, (8, 128), 0)
    lane = lax.broadcasted_iota(I32, (8, 128), 1)
    for b in (1, 2, 4):
        step = 16 * b
        sb = (sub & b) != 0
        lb = (lane & step) != 0
        down = roll(roll(x, 8 - b, 0), step, 1)
        up = roll(roll(x, b, 0), 128 - step, 1)
        x = jnp.where(sb == lb, x, jnp.where(sb, up, down))
    return x


def lag_tables(high_ref, low_ref, fine_ref):
    scale = 1.0 / math.sqrt(BINS * SEGS)
    lag = lax.broadcasted_iota(I32, (32, LAGS), 1) - LAGS // 2
    fine = ((lax.broadcasted_iota(I32, (32, LAGS), 0) * lag) & (NFFT - 1)).astype(F32) * (2.0 * math.pi / NFFT)
    fine_ref[0] = jnp.cos(fine)
    fine_ref[1] = jnp.sin(fine)
    lag1 = lax.broadcasted_iota(I32, (8, LAGS), 1) - LAGS // 2

    def rows(a, carry):
        coarse = ((lag1 * (32 * a)) & (NFFT - 1)).astype(F32) * (2.0 * math.pi / NFFT)
        cosine, sine = jnp.cos(coarse)[0:1] * scale, jnp.sin(coarse)[0:1] * scale
        at = pl.multiple_of(a * 32, 32)
        for part, value in ((0, cosine * fine_ref[0] - sine * fine_ref[1]),
                            (BINS, -(sine * fine_ref[0] + cosine * fine_ref[1]))):
            high = value.astype(BF16)
            high_ref[pl.ds(part + at, 32), :] = high
            low_ref[pl.ds(part + at, 32), :] = (value - high.astype(F32)).astype(BF16)
        return carry

    lax.fori_loop(0, BINS // 32, rows, 0)


def whiten_all(spec_ref, white):
    lane = lax.broadcasted_iota(I32, (STB, BINS), 1)

    def one(s, carry):
        x = spec_ref[s]
        power = jnp.sum(x * x, axis=0)
        total = power
        total += jnp.where(lane >= 1, roll(power, 1, 1), 0.0)
        total += jnp.where(lane >= 2, roll(power, 2, 1), 0.0)
        total += jnp.where(lane < BINS - 1, roll(power, BINS - 1, 1), 0.0)
        total += jnp.where(lane < BINS - 2, roll(power, BINS - 2, 1), 0.0)
        water = jnp.sum(power, axis=1, keepdims=True) * (1.0 / (3.0 * BINS))
        inv = 1.0 / jnp.sqrt(total * (1.0 / 15.0) + 0.25 * water + 1e-06)
        white[:, pl.ds(pl.multiple_of(s * STB, STB), STB), :] = x * inv[None]
        return carry

    lax.fori_loop(0, HS, one, 0)


def pack_bin(f, white, pack):
    for c in range(6):
        for half in range(2):
            cols = slice((2 * f + half) * 128, (2 * f + half) * 128 + 128)
            pack[f, pl.ds(half * 1024 + c, 128, stride=8), :] = white[c, :, cols].T


def resolve_stations(lout_ref, slots_ref, idx_ref):
    sends = lout_ref[:, 0, :].astype(F32)
    slots_ref[...] = jnp.concatenate([sends, jnp.zeros((64, 128), F32)], axis=0).T
    first = slots_ref[pl.ds(0, NT, stride=2), :]
    second = slots_ref[pl.ds(1, NT, stride=2), :]
    slot = lout_ref[:, 1, :]
    owner = jnp.maximum(slot, 0) // 2
    pick = jnp.where(slot % 2 == 0, jnp.take_along_axis(first, owner, axis=1),
                     jnp.take_along_axis(second, owner, axis=1))
    station = owner.astype(F32) * STB + pick
    station = jnp.where((slot < 0) | (pick >= STB), -1.0, station)
    for tg in range(8):
        idx_ref[tg] = swap_blocks(station[tg * 8:(tg + 1) * 8])


def build_selectors(idx_ref, hot):
    station = lax.broadcasted_iota(I32, (128, 256), 0)

    def one(i, carry):
        tg, h = i // NH, i % NH
        wanted = jnp.concatenate([idx_ref[tg, pl.ds(h, 1), :], idx_ref[tg, pl.ds(4 + h, 1), :]], axis=1).astype(I32)
        for k in range(8):
            hot[i, k * 128:k * 128 + 128, :] = (station == wanted - k * 128).astype(F32).astype(BF16)
        return carry

    lax.fori_loop(0, 32, one, 0)


def build_table(f, recv, table):
    sub = lax.broadcasted_iota(I32, (8, 128), 0)
    lane = lax.broadcasted_iota(I32, (8, 128), 1)
    l16, l32, l64 = (lane & 16) != 0, (lane & 32) != 0, (lane & 64) != 0
    same, top = ((sub & 4) != 0) == l16, (sub & 4) != 0

    def group(og, carry):
        for ci in range(3):
            parts = []
            for c in (2 * ci, 2 * ci + 1):
                v = []
                for g in range(4):
                    x = recv[f, pl.ds(og * 256 + g * 64 + c, 8, stride=8), :]
                    y = roll(x, 4, 0)
                    v.append(jnp.where(same, x, jnp.where(top, roll(y, 112, 1), roll(y, 16, 1))))
                w = [None] * 4
                for hi in range(2):
                    a, b = v[2 * hi], v[2 * hi + 1]
                    w[2 * hi] = jnp.where(l32, roll(b, 32, 1), a)
                    w[2 * hi + 1] = jnp.where(l32, b, roll(a, 96, 1))
                u = [None] * 4
                for lo in range(2):
                    a, b = w[lo], w[2 + lo]
                    u[lo] = jnp.where(l64, roll(b, 64, 1), a)
                    u[2 + lo] = jnp.where(l64, b, roll(a, 64, 1))
                parts.append(u)
            for sv in range(4):
                both = jnp.concatenate([parts[0][sv], parts[1][sv]], axis=0)
                high = both.astype(BF16)
                low = (both - high.astype(F32)).astype(BF16)
                row = (sv * 6 + 2 * ci) * 8
                cols = pl.ds(pl.multiple_of(og * 128, 128), 128)
                table[row:row + 16, cols] = high
                table[192 + row:192 + row + 16, cols] = low
        return carry

    lax.fori_loop(0, 8, group, 0)


def pair_sums(table, chosen, prod):
    full = jnp.dot(table[...], chosen, preferred_element_type=F32)
    prod[...] = full[:192] + full[192:]
    acc = [None] * 18
    for sv in range(4):
        rows = [slice((sv * 6 + c) * 8, (sv * 6 + c) * 8 + 8) for c in range(6)]
        a = [prod[r, 0:128] for r in rows]
        b = [prod[r, 128:256] for r in rows]
        for p in range(3):
            for q in range(3):
                re = a[2 * p] * b[2 * q] + a[2 * p + 1] * b[2 * q + 1]
                im = a[2 * p + 1] * b[2 * q] - a[2 * p] * b[2 * q + 1]
                n = (p * 3 + q) * 2
                acc[n] = re if sv == 0 else acc[n] + re
                acc[n + 1] = im if sv == 0 else acc[n + 1] + im
    return [jnp.sum(v, axis=0, keepdims=True) for v in acc]


def block_at(i):
    _, h, z, _ = position()
    return (z + 3 * (i + 1)) % 8, (h + i // 8 + 1) % NH


def correlate_kernel(spec_ref, lists_ref, out_ref, white, pack, recv, lout, slots_ref, idx_ref, hot, table, prod, half,
                     cross, got, high_ref, low_ref, fine_ref, sum_ref, plane_sem, all_sem, send_sem, recv_sem, own_sem,
                     lsend_sem, lrecv_sem, lown_sem, osend_sem, orecv_sem, oown_sem):
    t, h, _, _ = position()
    me, mine = t * NH + h, h * NT + t
    entry_barrier()
    whiten_all(spec_ref, white)
    pack_bin(0, white, pack)
    entry_barrier_rest(plane_sem, all_sem)

    def rows_of(d, n):
        return pl.ds(pl.multiple_of(d * 8, 8), n)

    def send_lists(t2, h2):
        pltpu.make_async_remote_copy(src_ref=lists_ref, dst_ref=lout.at[t], send_sem=lsend_sem, recv_sem=lrecv_sem,
                                     device_id=(t2, h2), device_id_type=MESH).start()

    each_peer(1, send_lists)
    lown = pltpu.make_async_copy(lists_ref, lout.at[t], lown_sem)
    lown.start()
    owns = []
    for f in range(2):
        def send(t2, h2, f=f):
            pltpu.make_async_remote_copy(src_ref=pack.at[f, rows_of(h2 * NT + t2, 6)], dst_ref=recv.at[f, rows_of(me, 6)],
                                         send_sem=send_sem.at[f], recv_sem=recv_sem.at[f], device_id=(t2, h2),
                                         device_id_type=MESH).start()

        if f == 1:
            pack_bin(1, white, pack)
        own = pltpu.make_async_copy(pack.at[f, rows_of(mine, 6)], recv.at[f, rows_of(me, 6)], own_sem.at[f])
        own.start()
        owns.append(own)
        each_peer(NH, send)
    lown.wait()
    lrest = pl.ds(0, NT - 1)
    pltpu.make_async_copy(lout.at[lrest], lout.at[lrest], lrecv_sem).wait()
    resolve_stations(lout, slots_ref, idx_ref)
    build_selectors(idx_ref, hot)
    lag_tables(high_ref, low_ref, fine_ref)
    rest = pl.ds(0, (ND - 1) * 6)

    def arrived(f):
        owns[f].wait()
        pltpu.make_async_copy(recv.at[f, rest], recv.at[f, rest], recv_sem.at[f]).wait()
        build_table(f, recv, table)

    arrived(0)

    def first(k, carry):
        for j in range(2):
            i = 2 * k + j
            sums = pair_sums(table, hot[i], prod.at[j])
            half[i, 0:18, :] = jnp.concatenate(sums, axis=0)
        return carry

    lax.fori_loop(0, 16, first, 0)
    arrived(1)

    def deliver(i):
        tg, h2 = block_at(i)
        for x in range(8):
            t2 = tg * 8 + x
            src, dst = cross.at[rows_of(h2 * NT + t2, RR)], got.at[rows_of(mine, RR)]

            @pl.when(h2 * NT + t2 != mine)
            def _():
                pltpu.make_async_remote_copy(src_ref=src, dst_ref=dst, send_sem=osend_sem, recv_sem=orecv_sem,
                                             device_id=(t2, h2), device_id_type=MESH).start()

            @pl.when(h2 * NT + t2 == mine)
            def _():
                pltpu.make_async_copy(src, dst, oown_sem).start()

    def second(k, carry):
        for j in range(2):
            i = 2 * k + j
            tg, h2 = block_at(i)
            sums = pair_sums(table, hot[tg * NH + h2], prod.at[j])
            before = half[tg * NH + h2]
            zero = jnp.zeros((4, 128), F32)
            parts = [before[0:8], before[8:16], jnp.concatenate([before[16:18]] + sums[0:6], axis=0),
                     jnp.concatenate(sums[6:14], axis=0), jnp.concatenate(sums[14:18] + [zero], axis=0)]
            for r in range(RR):
                cross[pl.ds((h2 * NT + tg * 8) * 8 + r, 8, stride=8), :] = swap_blocks(parts[r])
        for j in range(2):
            deliver(2 * k + j)
        return carry

    lax.fori_loop(0, 16, second, 0)
    pltpu.make_async_copy(cross.at[mine_rows(mine)], got.at[mine_rows(mine)], oown_sem).wait()
    orest = pl.ds(0, (ND - 1) * RR)
    pltpu.make_async_copy(got.at[orest], got.at[orest], orecv_sem).wait()
    for r in range(RR):
        turned = got[pl.ds(r, ND, stride=8), :].T
        for g in range(8):
            m = r * 8 + g
            if m < 36:
                f, c, ri = m // 18, m % 18 // 2, m % 2
                at = (ri * 2 + f) * 256
                sum_ref[c * 16:c * 16 + 16, at:at + 256] = turned[g * 16:g * 16 + 16]
    total = sum_ref[...]
    high = total.astype(BF16)
    low = (total - high.astype(F32)).astype(BF16)
    for j in range(4):
        cols = slice(j * 256, j * 256 + 256)
        part = jnp.dot(high, high_ref[:, cols], preferred_element_type=F32)
        part += jnp.dot(high, low_ref[:, cols], preferred_element_type=F32)
        part += jnp.dot(low, high_ref[:, cols], preferred_element_type=F32)
        for c in range(9):
            out_ref[:, c * LAGS + j * 256:c * LAGS + j * 256 + 256] = part[c * 16:c * 16 + 16]
    for f in range(2):
        pltpu.make_async_copy(pack.at[f, rest], pack.at[f, rest], send_sem.at[f]).wait()
    pltpu.make_async_copy(lout.at[lrest], lout.at[lrest], lsend_sem).wait()
    pltpu.make_async_copy(cross.at[orest], cross.at[orest], osend_sem).wait()


def mine_rows(mine):
    return pl.ds(pl.multiple_of(mine * 8, 8), RR)


def correlate(spectra, lists):
    vmem = pl.BlockSpec(memory_space=pltpu.VMEM)
    sem = pltpu.SemaphoreType
    return pl.pallas_call(
        correlate_kernel,
        out_shape=jax.ShapeDtypeStruct((16, 9 * LAGS), F32),
        in_specs=[vmem, vmem],
        out_specs=vmem,
        scratch_shapes=[
            pltpu.VMEM((6, HS * STB, BINS), F32), pltpu.VMEM((2, ND * 8, 128), F32), pltpu.VMEM((2, ND * 8, 128), F32),
            pltpu.VMEM((NT, 2, 128), I32), pltpu.VMEM((128, 128), F32), pltpu.VMEM((8, 8, 128), F32),
            pltpu.VMEM((32, 1024, 256), BF16), pltpu.VMEM((384, 1024), BF16), pltpu.VMEM((2, 192, 256), F32),
            pltpu.VMEM((32, 24, 128), F32), pltpu.VMEM((ND * 8, 128), F32), pltpu.VMEM((ND * 8, 128), F32),
            pltpu.VMEM((2 * BINS, LAGS), BF16), pltpu.VMEM((2 * BINS, LAGS), BF16), pltpu.VMEM((2, 32, LAGS), F32),
            pltpu.VMEM((144, 2 * BINS), F32), sem.REGULAR, sem.REGULAR, sem.DMA((2,)), sem.DMA((2,)), sem.DMA((2,)),
            sem.DMA, sem.DMA, sem.DMA, sem.DMA, sem.DMA, sem.DMA],
        compiler_params=pltpu.CompilerParams(collective_id=0, has_side_effects=True, vmem_limit_bytes=60 * 2**20),
        name="correlate",
    )(spectra, lists)


def body(spectra, send_list, pair_list, pair_count):
    pairs = pair_list[0]
    live = jnp.arange(pairs.shape[0], dtype=I32)[:, None] < pair_count[0]
    slots = jnp.where(live, pairs, -1).T.reshape(128)
    lists = jnp.stack([send_list[0].reshape(128), slots])
    return correlate(spectra, lists)


def solution(mesh):
    in_specs = (P("hour", None, "tile", None), P("tile", None, None), P("tile", None, None), P("tile"))
    return jax.shard_map(body, mesh=mesh, in_specs=in_specs, out_specs=P(("tile", "hour"), None), check_vma=False)
```

time: 410 us -> 85.3 us (0.21)
  waiting for transfers between devices: 301 us -> 0 us
  Pallas kernels: 0 us -> 80.3 us
  other arithmetic: 39.8 us -> 1.27 us
  local copies, waits for them, and re-layouts: 36.3 us -> 2.91 us
  between operations: 14.3 us -> 0.67 us
  starting transfers between devices: 13.5 us -> 0 us
  matrix products: 4.27 us -> 0 us
    all_to_all x1 -> x0, waiting for transfers between devices: 271 us -> none  [body(): lax.all_to_all(selected, 'tile', split_axis=2, concat_axis=2, tiled=True)]
    pallas_call x0 -> x1, Pallas kernels: none -> 80.3 us  [correlate(): pl.pallas_call(correlate_kernel, out_shape=jax.ShapeDtypeStruct((16, 9 *...]
    reduce_scatter x1 -> x0, waiting for transfers between devices: 30.2 us -> none  [body(): lax.psum_scatter(spectral_sum, 'hour', scatter_dimension=2, tiled=True)]
    mul x4 -> x0, other arithmetic: 23.2 us -> none  [the longest x1 12.1 us: body(): selected = jnp.take(whitened, chosen, axis=2) * used_scale]
    gather x3 -> x0, local copies, waits for them, and re-layouts: 22.2 us -> none  [the longest x1 8.13 us: pair_sums(): second_rows = jnp.take(pooled, second_slot, axis=2)]
    all_to_all x1 -> x0, starting transfers between devices: 13.3 us -> none  [body(): lax.all_to_all(selected, 'tile', split_axis=2, concat_axis=2, tiled=True)]
    all_to_all x1 -> x0, local copies, waits for them, and re-layouts: 11.3 us -> none  [body(): lax.all_to_all(selected, 'tile', split_axis=2, concat_axis=2, tiled=True)]
    reduce_sum x4 -> x0, other arithmetic: 9.84 us -> none  [the longest x3 8.25 us: pair_sums(): jnp.sum(first_real * second_real + first_imag * second_imag, axis=0)]
  transfers between devices with their start and end apart: 2 -> 0, of which waited for: 2 -> 0; matrix products, arithmetic and copies ran while one was open for 2% -> 0% of each run, Pallas kernels for 0% -> 0%
where the time goes in v2:
time: 85.3 us; the launch traced here: 85.2 us
  Pallas kernels  80.3 us (94%)
  local copies, waits for them, and re-layouts  2.91 us (3%)
  other arithmetic  1.27 us (1%)
    pallas_call x1, Pallas kernels, correlate(): pl.pallas_call(correlate_kernel, out_shape=jax.ShapeDtypeStruct((16, 9 *...  80.3 us
    unnamed x2, local copies, waits for them, and re-layouts  2.69 us

profile of v2, /device:TPU:1, one launch (start us, length us, event | category | flops | bytes accessed | tf_op | source)
XLA Modules:
  0.0 85.2 jit_solution(6807516625748300873)
XLA Ops:
  0.7 0.7 fusion
  1.4 0.1 stack_reshape.3
  1.4 0.8 copy.6
  2.2 0.1 stack_reshape_squeeze.3
  2.3 0.6 pad_add_fusion.lists_ref
  2.9 80.3 %correlate.1 = f32[16,9216]{1,0:T(8,128)} custom-call(f32[8,6,16,512]{3,2,1,0:T(8,128)} %spec_ref.1, s32[2,128]{1,0:T(2,128)} %pad_add_fusion.lists_ref), custom_call_target="tpu_custom_call" | custom-call | tf_op jit(solution)/shard_map/correlate/pallas_call | solution.py:349
  83.2 1.9 %copy.9 = f32[16,9216]{1,0:T(8,128)} copy(f32[16,9216]{1,0:T(8,128)} %correlate.1) | data formatting | bytes 1179648
  (1 shorter events, 0.0 us)

commit v3 on v2

v3 whole, which is shorter than its diff:
```python
import functools
import math

import jax
import jax.numpy as jnp
from jax import lax
from jax.experimental import pallas as pl
from jax.experimental.pallas import tpu as pltpu
from jax.sharding import PartitionSpec as P

MESH = pl.DeviceIdType.MESH
F32, BF16, I32 = jnp.float32, jnp.bfloat16, jnp.int32

NFFT = 2048
LAGS = 1024
BINS = 512
SEGS = 32
HS = 8
STB = 16
NT, NH = 64, 4
ND = NT * NH
CH = 12
RR = 3


def position():
    t = lax.axis_index("tile")
    return t, lax.axis_index("hour"), t // 8, t % 8


def entry_barrier():
    t, h, z, xc = position()
    bar = pltpu.get_barrier_semaphore()
    for i in range(1, 8):
        pl.semaphore_signal(bar, inc=1, device_id=(((z + i) % 8) * 8 + xc, h), device_id_type=MESH)
    for i in range(1, 8):
        pl.semaphore_signal(bar, inc=1, device_id=(z * 8 + (xc + i) % 8, h), device_id_type=MESH)
    for i in range(1, NH):
        pl.semaphore_signal(bar, inc=1, device_id=(t, (h + i) % NH), device_id_type=MESH)


def barrier_rounds(plane_sem, all_sem, plane_act, act):
    t, h, z, xc = position()
    pl.semaphore_wait(pltpu.get_barrier_semaphore(), 17)
    others = [z * 8 + (xc + i) % 8 for i in range(1, 8)]
    for t2 in others:
        pl.semaphore_signal(plane_sem, inc=1, device_id=(t2, h), device_id_type=MESH)
    near = [(z + d) % 8 * 8 + xc for d in (4, 3, 5, 2, 6, 1, 7)] + others
    for one in (plane_act, act):
        for t2 in near:
            one(t2, h)
    for i in range(1, NH):
        act(t, (h + i) % NH)
    pl.semaphore_wait(plane_sem, 7)
    for i in range(1, NH):
        pl.semaphore_signal(all_sem, inc=1, device_id=(t, (h + i) % NH), device_id_type=MESH)
    zs = [((z + d) % 8) * 8 for d in (4, 3, 5, 2, 6, 1, 7, 0)]

    for one in (plane_act, act):
        def plane(i, carry, one=one):
            xc2 = (xc + i) % 8
            for base in zs[:7]:
                one(base + xc2, h)
            return carry

        lax.fori_loop(1, 8, plane, 0)
    pl.semaphore_wait(all_sem, NH - 1)

    def rest(k, carry):
        xc2, h2 = (xc + k) % 8, (h + k // 8) % NH
        for n, base in enumerate(zs):
            if n < 7:
                act(base + xc2, h2)
            else:
                pl.when(k % 8 > 0)(lambda: act(base + xc2, h2))
        return carry

    lax.fori_loop(8, 8 * NH, rest, 0)


def each_peer(planes, act):
    t, h, z, xc = position()
    zs = [((z + d) % 8) * 8 for d in range(8)]
    cs = [(xc + d) % 2 for d in range(2)]

    def some(k, carry):
        x2, h2 = ((xc // 2 + k) % 4) * 2, (h + k // 4) % NH
        for dz in range(8):
            for dc in range(2):
                if dz + dc == 0:
                    pl.when(k > 0)(lambda: act(zs[0] + x2 + cs[0], h2))
                else:
                    act(zs[dz] + x2 + cs[dc], h2)
        return carry

    lax.fori_loop(0, 4 * planes, some, 0)


def roll(x, shift, axis):
    return pltpu.roll(x, shift, axis)


def swap_blocks(x):
    sub = lax.broadcasted_iota(I32, (8, 128), 0)
    lane = lax.broadcasted_iota(I32, (8, 128), 1)
    for b in (1, 2, 4):
        step = 16 * b
        sb = (sub & b) != 0
        lb = (lane & step) != 0
        down = roll(roll(x, 8 - b, 0), step, 1)
        up = roll(roll(x, b, 0), 128 - step, 1)
        x = jnp.where(sb == lb, x, jnp.where(sb, up, down))
    return x


def lag_tables(high_ref, low_ref, fine_ref):
    scale = 1.0 / math.sqrt(BINS * SEGS)
    lag = lax.broadcasted_iota(I32, (32, LAGS), 1) - LAGS // 2
    fine = ((lax.broadcasted_iota(I32, (32, LAGS), 0) * lag) & (NFFT - 1)).astype(F32) * (2.0 * math.pi / NFFT)
    fine_ref[0] = jnp.cos(fine)
    fine_ref[1] = jnp.sin(fine)
    lag1 = lax.broadcasted_iota(I32, (8, LAGS), 1) - LAGS // 2

    def rows(a, carry):
        coarse = ((lag1 * (32 * a)) & (NFFT - 1)).astype(F32) * (2.0 * math.pi / NFFT)
        cosine, sine = jnp.cos(coarse)[0:1] * scale, jnp.sin(coarse)[0:1] * scale
        at = pl.multiple_of(a % 8 * 32, 32)
        for part, value in ((0, cosine * fine_ref[0] - sine * fine_ref[1]),
                            (256, -(sine * fine_ref[0] + cosine * fine_ref[1]))):
            high = value.astype(BF16)
            high_ref[a // 8, pl.ds(part + at, 32), :] = high
            low_ref[a // 8, pl.ds(part + at, 32), :] = (value - high.astype(F32)).astype(BF16)
        return carry

    lax.fori_loop(0, BINS // 32, rows, 0)


def rows_of(d, n):
    return pl.ds(pl.multiple_of(d * 8, 8), n)


def whiten_all(spec_ref, white):
    lane = lax.broadcasted_iota(I32, (STB, BINS), 1)

    def one(s, carry):
        x = spec_ref[s]
        power = jnp.sum(x * x, axis=0)
        total = power
        total += jnp.where(lane >= 1, roll(power, 1, 1), 0.0)
        total += jnp.where(lane >= 2, roll(power, 2, 1), 0.0)
        total += jnp.where(lane < BINS - 1, roll(power, BINS - 1, 1), 0.0)
        total += jnp.where(lane < BINS - 2, roll(power, BINS - 2, 1), 0.0)
        water = jnp.sum(power, axis=1, keepdims=True) * (1.0 / (3.0 * BINS))
        inv = 1.0 / jnp.sqrt(total * (1.0 / 15.0) + 0.25 * water + 1e-06)
        white[:, pl.ds(pl.multiple_of(s * STB, STB), STB), :] = x * inv[None]
        return carry

    lax.fori_loop(0, HS, one, 0)


def pack_bin(f, white, pack):
    for c in range(6):
        for half in range(2):
            cols = slice((2 * f + half) * 128, (2 * f + half) * 128 + 128)
            pack[f, pl.ds(half * 1024 + c, 128, stride=8), :] = white[c, :, cols].T


def pack_lists(send_ref, pair_ref, count_ref, lists):
    live = lax.broadcasted_iota(I32, (2, 64), 1) < count_ref[0]
    pairs = jnp.where(live, pair_ref[...], -1)
    sends = send_ref[...]
    for j in range(2):
        lists[0:1, j * 64:j * 64 + 64] = sends[j:j + 1]
        lists[1:2, j * 64:j * 64 + 64] = pairs[j:j + 1]


def resolve_stations(lout_ref, slots_ref, idx_ref):
    sends = lout_ref[:, 0, :].astype(F32)
    slots_ref[...] = jnp.concatenate([sends, jnp.zeros((64, 128), F32)], axis=0).T
    first, second = slots_ref[0:NT, :], slots_ref[NT:2 * NT, :]
    slot = lout_ref[:, 1, :]
    owner = jnp.maximum(slot, 0) // 2
    pick = jnp.where(slot % 2 == 0, jnp.take_along_axis(first, owner, axis=1),
                     jnp.take_along_axis(second, owner, axis=1))
    station = owner.astype(F32) * STB + pick
    station = jnp.where((slot < 0) | (pick >= STB), -1.0, station)
    for tg in range(8):
        idx_ref[tg] = swap_blocks(station[tg * 8:(tg + 1) * 8])


def build_selectors(idx_ref, hot):
    station = lax.broadcasted_iota(I32, (128, 256), 0)

    def one(i, carry):
        tg, h = i // NH, i % NH
        wanted = jnp.concatenate([idx_ref[tg, pl.ds(h, 1), :], idx_ref[tg, pl.ds(4 + h, 1), :]], axis=1).astype(I32)
        for k in range(8):
            hot[i, k * 128:k * 128 + 128, :] = (station == wanted - k * 128).astype(F32).astype(BF16)
        return carry

    lax.fori_loop(0, 32, one, 0)


def build_table(f, recv, table):
    sub = lax.broadcasted_iota(I32, (8, 128), 0)
    lane = lax.broadcasted_iota(I32, (8, 128), 1)
    l16, l32, l64 = (lane & 16) != 0, (lane & 32) != 0, (lane & 64) != 0
    same, top = ((sub & 4) != 0) == l16, (sub & 4) != 0

    def one(og):
        for ci in range(3):
            parts = []
            for c in (2 * ci, 2 * ci + 1):
                v = []
                for g in range(4):
                    x = recv[f, pl.ds(og * 256 + g * 64 + c, 8, stride=8), :]
                    y = roll(x, 4, 0)
                    v.append(jnp.where(same, x, jnp.where(top, roll(y, 112, 1), roll(y, 16, 1))))
                w = [None] * 4
                for hi in range(2):
                    a, b = v[2 * hi], v[2 * hi + 1]
                    w[2 * hi] = jnp.where(l32, roll(b, 32, 1), a)
                    w[2 * hi + 1] = jnp.where(l32, b, roll(a, 96, 1))
                u = [None] * 4
                for lo in range(2):
                    a, b = w[lo], w[2 + lo]
                    u[lo] = jnp.where(l64, roll(b, 64, 1), a)
                    u[2 + lo] = jnp.where(l64, b, roll(a, 64, 1))
                parts.append(u)
            for sv in range(4):
                both = jnp.concatenate([parts[0][sv], parts[1][sv]], axis=0)
                high = both.astype(BF16)
                low = (both - high.astype(F32)).astype(BF16)
                row = (sv * 6 + 2 * ci) * 8
                cols = pl.ds(pl.multiple_of(og * 128, 128), 128)
                table[row:row + 16, cols] = high
                table[192 + row:192 + row + 16, cols] = low

    def some(k, carry):
        for j in range(4):
            one(4 * k + j)
        return carry

    lax.fori_loop(0, 2, some, 0)


def select_pairs(table, chosen, prod):
    full = jnp.dot(table[...], chosen, preferred_element_type=F32)
    prod[...] = full[:192] + full[192:]


def pair_sums(prod):
    acc = [None] * 18
    for sv in range(4):
        rows = [slice((sv * 6 + c) * 8, (sv * 6 + c) * 8 + 8) for c in range(6)]
        a = [prod[r, 0:128] for r in rows]
        b = [prod[r, 128:256] for r in rows]
        for p in range(3):
            for q in range(3):
                re = a[2 * p] * b[2 * q] + a[2 * p + 1] * b[2 * q + 1]
                im = a[2 * p + 1] * b[2 * q] - a[2 * p] * b[2 * q + 1]
                n = (p * 3 + q) * 2
                acc[n] = re if sv == 0 else acc[n] + re
                acc[n + 1] = im if sv == 0 else acc[n + 1] + im
    return [jnp.sum(v, axis=0, keepdims=True) for v in acc]


def block_at(i):
    _, h, z, _ = position()
    return (z + 3 * (i + 1)) % 8, (h + i // 8 + 1) % NH


def correlate_kernel(spec_hbm, slist_ref, plist_ref, count_ref, out_ref, spec_ref, lists_ref, white, pack, recv, lout, slots_ref, idx_ref, hot, table, prod0, prod1,
                     cross, got, high_ref, low_ref, fine_ref, sum_ref, plane_sem, all_sem, send_sem, recv_sem, own_sem,
                     lsend_sem, lrecv_sem, lown_sem, osend_sem, orecv_sem, oown_sem, fetch_sem):
    t, h, _, _ = position()
    me, mine = t * NH + h, h * NT + t
    fetch = pltpu.make_async_copy(spec_hbm, spec_ref, fetch_sem)
    fetch.start()
    entry_barrier()
    pack_lists(slist_ref, plist_ref, count_ref, lists_ref)
    fetch.wait()
    whiten_all(spec_ref, white)
    pack_bin(0, white, pack)
    owns = [pltpu.make_async_copy(pack.at[f, rows_of(mine, 6)], recv.at[f, rows_of(me, 6)], own_sem.at[f])
            for f in range(2)]

    def send(f, t2, h2):
        pltpu.make_async_remote_copy(src_ref=pack.at[f, rows_of(h2 * NT + t2, 6)], dst_ref=recv.at[f, rows_of(me, 6)],
                                     send_sem=send_sem.at[f], recv_sem=recv_sem.at[f], device_id=(t2, h2),
                                     device_id_type=MESH).start()

    def send_lists(t2, h2):
        pltpu.make_async_remote_copy(src_ref=lists_ref, dst_ref=lout.at[t], send_sem=lsend_sem, recv_sem=lrecv_sem,
                                     device_id=(t2, h2), device_id_type=MESH).start()

    barrier_rounds(plane_sem, all_sem, send_lists, functools.partial(send, 0))
    lown = pltpu.make_async_copy(lists_ref, lout.at[t], lown_sem)
    lown.start()
    owns[0].start()
    pack_bin(1, white, pack)
    owns[1].start()
    each_peer(NH, functools.partial(send, 1))
    lag_tables(high_ref, low_ref, fine_ref)
    lown.wait()
    lrest = pl.ds(0, NT - 1)
    pltpu.make_async_copy(lout.at[lrest], lout.at[lrest], lrecv_sem).wait()
    resolve_stations(lout, slots_ref, idx_ref)
    build_selectors(idx_ref, hot)
    rest = pl.ds(0, (ND - 1) * 6)

    def arrived(f):
        owns[f].wait()
        pltpu.make_async_copy(recv.at[f, rest], recv.at[f, rest], recv_sem.at[f]).wait()
        build_table(f, recv, table)

    def place(i):
        tg, h2 = block_at(i)
        return tg * NH + h2

    def deliver(f, i, last=False):
        tg, h2 = block_at(i)
        for x in range(8):
            t2 = tg * 8 + x
            src, dst = cross.at[f, rows_of(h2 * NT + t2, RR)], got.at[f, rows_of(mine, RR)]
            copy = pltpu.make_async_remote_copy(src_ref=src, dst_ref=dst, send_sem=osend_sem.at[f],
                                                recv_sem=orecv_sem.at[f], device_id=(t2, h2), device_id_type=MESH)
            if last:
                pl.when(t2 != t)(copy.start)
            else:
                copy.start()

    def finish(f, i, sums):
        tg, h2 = block_at(i)
        zero = jnp.zeros((6, 128), F32)
        for r in range(RR):
            part = jnp.concatenate(sums[r * 8:r * 8 + 8] if r < 2 else sums[16:18] + [zero], axis=0)
            cross[f, pl.ds((h2 * NT + tg * 8) * 8 + r, 8, stride=8), :] = swap_blocks(part)

    def blocks(f):
        select_pairs(table, hot[place(0)], prod0)

        def two(k, carry):
            i = 2 * k
            select_pairs(table, hot[place(i + 1)], prod1)
            finish(f, i, pair_sums(prod0))
            select_pairs(table, hot[place(jnp.minimum(i + 2, 31))], prod0)
            finish(f, i + 1, pair_sums(prod1))
            deliver(f, i)
            pl.when(k < 15)(lambda: deliver(f, i + 1))
            return carry

        lax.fori_loop(0, 16, two, 0)
        deliver(f, 31, last=True)
        pltpu.make_async_copy(cross.at[f, rows_of(mine, RR)], got.at[f, rows_of(mine, RR)], oown_sem.at[f]).start()

    orest = pl.ds(0, (ND - 1) * RR)

    def transform(f):
        pltpu.make_async_copy(cross.at[f, rows_of(mine, RR)], got.at[f, rows_of(mine, RR)], oown_sem.at[f]).wait()
        pltpu.make_async_copy(got.at[f, orest], got.at[f, orest], orecv_sem.at[f]).wait()
        for r in range(RR):
            turned = got[f, pl.ds(r, ND, stride=8), :].T
            for g in range(8 if r < 2 else 2):
                c, ri = (r * 8 + g) // 2, g % 2
                sum_ref[c * 16:c * 16 + 16, ri * 256:ri * 256 + 256] = turned[g * 16:g * 16 + 16]
        total = sum_ref[...]
        high = total.astype(BF16)
        low = (total - high.astype(F32)).astype(BF16)
        for j in range(4):
            cols = slice(j * 256, j * 256 + 256)
            wh, wl = high_ref[f, :, cols], low_ref[f, :, cols]
            part = jnp.dot(high, wh, preferred_element_type=F32)
            part += jnp.dot(high, wl, preferred_element_type=F32)
            part += jnp.dot(low, wh, preferred_element_type=F32)
            for c in range(9):
                at = slice(c * LAGS + j * 256, c * LAGS + j * 256 + 256)
                piece = part[c * 16:c * 16 + 16]
                out_ref[:, at] = piece if f == 0 else out_ref[:, at] + piece

    arrived(0)
    blocks(0)
    arrived(1)
    blocks(1)
    transform(0)
    transform(1)
    for f in range(2):
        pltpu.make_async_copy(pack.at[f, rest], pack.at[f, rest], send_sem.at[f]).wait()
        pltpu.make_async_copy(cross.at[f, orest], cross.at[f, orest], osend_sem.at[f]).wait()
    pltpu.make_async_copy(lout.at[lrest], lout.at[lrest], lsend_sem).wait()


def correlate(spectra, send_list, pair_list, pair_count):
    vmem = pl.BlockSpec(memory_space=pltpu.VMEM)
    sem = pltpu.SemaphoreType
    return pl.pallas_call(
        correlate_kernel,
        out_shape=jax.ShapeDtypeStruct((16, 9 * LAGS), F32),
        in_specs=[pl.BlockSpec(memory_space=pl.ANY), vmem, vmem, pl.BlockSpec(memory_space=pltpu.SMEM)],
        out_specs=vmem,
        scratch_shapes=[
            pltpu.VMEM((HS, 6, STB, BINS), F32), pltpu.VMEM((2, 128), I32),
            pltpu.VMEM((6, HS * STB, BINS), F32), pltpu.VMEM((2, ND * 8, 128), F32), pltpu.VMEM((2, ND * 8, 128), F32),
            pltpu.VMEM((NT, 2, 128), I32), pltpu.VMEM((128, 128), F32), pltpu.VMEM((8, 8, 128), F32),
            pltpu.VMEM((32, 1024, 256), BF16), pltpu.VMEM((384, 1024), BF16), pltpu.VMEM((192, 256), F32), pltpu.VMEM((192, 256), F32),
            pltpu.VMEM((2, ND * 8, 128), F32), pltpu.VMEM((2, ND * 8, 128), F32),
            pltpu.VMEM((2, BINS, LAGS), BF16), pltpu.VMEM((2, BINS, LAGS), BF16), pltpu.VMEM((2, 32, LAGS), F32),
            pltpu.VMEM((144, BINS), F32), sem.REGULAR, sem.REGULAR, sem.DMA((2,)), sem.DMA((2,)), sem.DMA((2,)),
            sem.DMA, sem.DMA, sem.DMA, sem.DMA((2,)), sem.DMA((2,)), sem.DMA((2,)), sem.DMA],
        compiler_params=pltpu.CompilerParams(collective_id=0, has_side_effects=True, vmem_limit_bytes=60 * 2**20),
        name="correlate",
    )(spectra, send_list, pair_list, pair_count)


def body(spectra, send_list, pair_list, pair_count):
    return correlate(spectra, send_list[0].T, pair_list[0].T, pair_count)


def solution(mesh):
    in_specs = (P("hour", None, "tile", None), P("tile", None, None), P("tile", None, None), P("tile"))
    return jax.shard_map(body, mesh=mesh, in_specs=in_specs, out_specs=P(("tile", "hour"), None), check_vma=False)
```

time: 85.3 us -> 80.6 us (0.945)
  Pallas kernels: 80.3 us -> 77.9 us
  other arithmetic: 1.27 us -> 0 us
  local copies, waits for them, and re-layouts: 2.91 us -> 1.92 us
    pallas_call x1, Pallas kernels: 80.3 us -> 77.9 us  [correlate(): pl.pallas_call(correlate_kernel, out_shape=jax.ShapeDtypeStruct((16, 9 *...]
    unnamed x2 -> x1, local copies, waits for them, and re-layouts: 2.69 us -> 1.92 us
where the time goes in v3:
time: 80.6 us; the launch traced here: 80.5 us
  Pallas kernels  77.9 us (97%)
  local copies, waits for them, and re-layouts  1.92 us (2%)
    pallas_call x1, Pallas kernels, correlate(): pl.pallas_call(correlate_kernel, out_shape=jax.ShapeDtypeStruct((16, 9 *...  77.9 us
    unnamed x1, local copies, waits for them, and re-layouts  1.92 us

profile of v3, /device:TPU:1, one launch (start us, length us, event | category | flops | bytes accessed | tf_op | source)
XLA Modules:
  0.0 80.5 jit_solution(18078868547592426119)
XLA Ops:
  0.7 77.9 %correlate.1 = f32[16,9216]{1,0:T(8,128)} custom-call(f32[8,6,16,512]{3,2,1,0:T(8,128)} %spec_hbm.1, s32[2,64]{1,0:T(2,128)} %bitcast.6, s32[2,64]{1,0:T(2,128)} %bitcast.7, s32[1]{0:T(128)S(6)} %copy.6.count_ref), custom_call_target="tpu_custom_call" | custom-call | tf_op jit(solution)/shard_map/correlate/pallas_call | solution.py:396
  78.6 1.9 %copy.7 = f32[16,9216]{1,0:T(8,128)} copy(f32[16,9216]{1,0:T(8,128)} %correlate.1) | data formatting | bytes 1179648

commit v4 on v3

--- a/solution.py
+++ b/solution.py
@@ -20,6 +20,7 @@
 NT, NH = 64, 4
 ND = NT * NH
 CH = 12
+UNROLL = 4
 RR = 3
 
 
@@ -338,20 +339,23 @@
             cross[f, pl.ds((h2 * NT + tg * 8) * 8 + r, 8, stride=8), :] = swap_blocks(part)
 
     def blocks(f):
+        prods = (prod0, prod1)
+
+        def some(i, last=False):
+            for j in range(UNROLL):
+                if not last or j < UNROLL - 1:
+                    select_pairs(table, hot[place(i + j + 1)], prods[(j + 1) % 2])
+                finish(f, i + j, pair_sums(prods[j % 2]))
+            for j in range(UNROLL):
+                deliver(f, i + j, last and j == UNROLL - 1)
+
+        def step(k, carry):
+            some(UNROLL * k)
+            return carry
+
         select_pairs(table, hot[place(0)], prod0)
-
-        def two(k, carry):
-            i = 2 * k
-            select_pairs(table, hot[place(i + 1)], prod1)
-            finish(f, i, pair_sums(prod0))
-            select_pairs(table, hot[place(jnp.minimum(i + 2, 31))], prod0)
-            finish(f, i + 1, pair_sums(prod1))
-            deliver(f, i)
-            pl.when(k < 15)(lambda: deliver(f, i + 1))
-            return carry
-
-        lax.fori_loop(0, 16, two, 0)
-        deliver(f, 31, last=True)
+        lax.fori_loop(0, 32 // UNROLL - 1, step, 0)
+        some(32 - UNROLL, last=True)
         pltpu.make_async_copy(cross.at[f, rows_of(mine, RR)], got.at[f, rows_of(mine, RR)], oown_sem.at[f]).start()
 
     orest = pl.ds(0, (ND - 1) * RR)
@@ -395,7 +399,7 @@
     sem = pltpu.SemaphoreType
     return pl.pallas_call(
         correlate_kernel,
-        out_shape=jax.ShapeDtypeStruct((16, 9 * LAGS), F32),
+        out_shape=pltpu.VMEM((16, 9 * LAGS), F32),
         in_specs=[pl.BlockSpec(memory_space=pl.ANY), vmem, vmem, pl.BlockSpec(memory_space=pltpu.SMEM)],
         out_specs=vmem,
         scratch_shapes=[

time: 80.6 us -> 77 us (0.955)
  Pallas kernels: 77.9 us -> 75.4 us
  local copies, waits for them, and re-layouts: 1.92 us -> 0.82 us
    pallas_call x1, Pallas kernels: 77.9 us -> 75.4 us  [correlate(): pl.pallas_call(correlate_kernel, out_shape=pltpu.VMEM((16, 9 * LAGS), F32...]
    unnamed x1, local copies, waits for them, and re-layouts: 1.92 us -> 0.82 us
where the time goes in v4:
time: 77 us; the launch traced here: 76.9 us
  Pallas kernels  75.4 us (98%)
  local copies, waits for them, and re-layouts  0.82 us (1%)
    pallas_call x1, Pallas kernels, correlate(): pl.pallas_call(correlate_kernel, out_shape=pltpu.VMEM((16, 9 * LAGS), F32...  75.4 us

profile of v4, /device:TPU:1, one launch (start us, length us, event | category | flops | bytes accessed | tf_op | source)
XLA Modules:
  0.0 76.9 jit_solution(12323963113090248960)
XLA Ops:
  0.7 75.4 %correlate.1 = f32[16,9216]{1,0:T(8,128)S(1)} custom-call(f32[8,6,16,512]{3,2,1,0:T(8,128)} %spec_hbm.1, s32[2,64]{1,0:T(2,128)} %bitcast.6, s32[2,64]{1,0:T(2,128)} %bitcast.7, s32[1]{0:T(128)S(6)} %copy.7.count_ref), custom_call_target="tpu_custom_call" | custom-call | tf_op jit(solution)/shard_map/correlate/pallas_call | solution.py:400
  76.1 0.8 %copy.6 = f32[16,9216]{1,0:T(8,128)} copy(f32[16,9216]{1,0:T(8,128)S(1)} %correlate.1) | data formatting | bytes 1179648

commit v5 on v4

--- a/solution.py
+++ b/solution.py
@@ -9,7 +9,8 @@
 from jax.sharding import PartitionSpec as P
 
 MESH = pl.DeviceIdType.MESH
-F32, BF16, I32 = jnp.float32, jnp.bfloat16, jnp.int32
+F32, BF16, I32, F8 = jnp.float32, jnp.bfloat16, jnp.int32, jnp.float8_e5m2
+LOW = 2.0 ** 22
 
 NFFT = 2048
 LAGS = 1024
@@ -189,20 +190,22 @@
         idx_ref[tg] = swap_blocks(station[tg * 8:(tg + 1) * 8])
 
 
-def build_selectors(idx_ref, hot):
+def build_selectors(idx_ref, hot, hot8):
     station = lax.broadcasted_iota(I32, (128, 256), 0)
 
     def one(i, carry):
         tg, h = i // NH, i % NH
         wanted = jnp.concatenate([idx_ref[tg, pl.ds(h, 1), :], idx_ref[tg, pl.ds(4 + h, 1), :]], axis=1).astype(I32)
         for k in range(8):
-            hot[i, k * 128:k * 128 + 128, :] = (station == wanted - k * 128).astype(F32).astype(BF16)
+            one_hot = (station == wanted - k * 128).astype(F32)
+            hot[i, k * 128:k * 128 + 128, :] = one_hot.astype(BF16)
+            hot8[i, k * 128:k * 128 + 128, :] = one_hot.astype(F8)
         return carry
 
     lax.fori_loop(0, 32, one, 0)
 
 
-def build_table(f, recv, table):
+def build_table(f, recv, table, low_table):
     sub = lax.broadcasted_iota(I32, (8, 128), 0)
     lane = lax.broadcasted_iota(I32, (8, 128), 1)
     l16, l32, l64 = (lane & 16) != 0, (lane & 32) != 0, (lane & 64) != 0
@@ -228,32 +231,27 @@
                     u[lo] = jnp.where(l64, roll(b, 64, 1), a)
                     u[2 + lo] = jnp.where(l64, b, roll(a, 64, 1))
                 parts.append(u)
-            for sv in range(4):
-                both = jnp.concatenate([parts[0][sv], parts[1][sv]], axis=0)
+            for sv in (0, 2):
+                both = jnp.concatenate([parts[0][sv], parts[1][sv], parts[0][sv + 1], parts[1][sv + 1]], axis=0)
                 high = both.astype(BF16)
-                low = (both - high.astype(F32)).astype(BF16)
-                row = (sv * 6 + 2 * ci) * 8
-                cols = pl.ds(pl.multiple_of(og * 128, 128), 128)
-                table[row:row + 16, cols] = high
-                table[192 + row:192 + row + 16, cols] = low
-
-    def some(k, carry):
-        for j in range(4):
-            one(4 * k + j)
-        return carry
-
-    lax.fori_loop(0, 2, some, 0)
-
-
-def select_pairs(table, chosen, prod):
-    full = jnp.dot(table[...], chosen, preferred_element_type=F32)
-    prod[...] = full[:192] + full[192:]
+                row = ci * 64 + sv * 16
+                cols = slice(og * 128, og * 128 + 128)
+                table[row:row + 32, cols] = high
+                low_table[row:row + 32, cols] = ((both - high.astype(F32)) * LOW).astype(F8)
+
+    for og in range(8):
+        one(og)
+
+
+def select_pairs(table, low_table, chosen, chosen8, prod):
+    high = jnp.dot(table[...], chosen, preferred_element_type=F32)
+    prod[...] = high + jnp.dot(low_table[...], chosen8, preferred_element_type=F32) * (1.0 / LOW)
 
 
 def pair_sums(prod):
     acc = [None] * 18
     for sv in range(4):
-        rows = [slice((sv * 6 + c) * 8, (sv * 6 + c) * 8 + 8) for c in range(6)]
+        rows = [slice(c // 2 * 64 + sv * 16 + c % 2 * 8, c // 2 * 64 + sv * 16 + c % 2 * 8 + 8) for c in range(6)]
         a = [prod[r, 0:128] for r in rows]
         b = [prod[r, 128:256] for r in rows]
         for p in range(3):
@@ -271,7 +269,7 @@
     return (z + 3 * (i + 1)) % 8, (h + i // 8 + 1) % NH
 
 
-def correlate_kernel(spec_hbm, slist_ref, plist_ref, count_ref, out_ref, spec_ref, lists_ref, white, pack, recv, lout, slots_ref, idx_ref, hot, table, prod0, prod1,
+def correlate_kernel(spec_hbm, slist_ref, plist_ref, count_ref, out_ref, spec_ref, lists_ref, white, pack, recv, lout, slots_ref, idx_ref, hot, hot8, table, low_table, prod0, prod1,
                      cross, got, high_ref, low_ref, fine_ref, sum_ref, plane_sem, all_sem, send_sem, recv_sem, own_sem,
                      lsend_sem, lrecv_sem, lown_sem, osend_sem, orecv_sem, oown_sem, fetch_sem):
     t, h, _, _ = position()
@@ -307,13 +305,13 @@
     lrest = pl.ds(0, NT - 1)
     pltpu.make_async_copy(lout.at[lrest], lout.at[lrest], lrecv_sem).wait()
     resolve_stations(lout, slots_ref, idx_ref)
-    build_selectors(idx_ref, hot)
+    build_selectors(idx_ref, hot, hot8)
     rest = pl.ds(0, (ND - 1) * 6)
 
     def arrived(f):
         owns[f].wait()
         pltpu.make_async_copy(recv.at[f, rest], recv.at[f, rest], recv_sem.at[f]).wait()
-        build_table(f, recv, table)
+        build_table(f, recv, table, low_table)
 
     def place(i):
         tg, h2 = block_at(i)
@@ -344,7 +342,7 @@
         def some(i, last=False):
             for j in range(UNROLL):
                 if not last or j < UNROLL - 1:
-                    select_pairs(table, hot[place(i + j + 1)], prods[(j + 1) % 2])
+                    select_pairs(table, low_table, hot[place(i + j + 1)], hot8[place(i + j + 1)], prods[(j + 1) % 2])
                 finish(f, i + j, pair_sums(prods[j % 2]))
             for j in range(UNROLL):
                 deliver(f, i + j, last and j == UNROLL - 1)
@@ -353,7 +351,7 @@
             some(UNROLL * k)
             return carry
 
-        select_pairs(table, hot[place(0)], prod0)
+        select_pairs(table, low_table, hot[place(0)], hot8[place(0)], prod0)
         lax.fori_loop(0, 32 // UNROLL - 1, step, 0)
         some(32 - UNROLL, last=True)
         pltpu.make_async_copy(cross.at[f, rows_of(mine, RR)], got.at[f, rows_of(mine, RR)], oown_sem.at[f]).start()
@@ -406,7 +404,7 @@
             pltpu.VMEM((HS, 6, STB, BINS), F32), pltpu.VMEM((2, 128), I32),
             pltpu.VMEM((6, HS * STB, BINS), F32), pltpu.VMEM((2, ND * 8, 128), F32), pltpu.VMEM((2, ND * 8, 128), F32),
             pltpu.VMEM((NT, 2, 128), I32), pltpu.VMEM((128, 128), F32), pltpu.VMEM((8, 8, 128), F32),
-            pltpu.VMEM((32, 1024, 256), BF16), pltpu.VMEM((384, 1024), BF16), pltpu.VMEM((192, 256), F32), pltpu.VMEM((192, 256), F32),
+            pltpu.VMEM((32, 1024, 256), BF16), pltpu.VMEM((32, 1024, 256), F8), pltpu.VMEM((192, 1024), BF16), pltpu.VMEM((192, 1024), F8), pltpu.VMEM((192, 256), F32), pltpu.VMEM((192, 256), F32),
             pltpu.VMEM((2, ND * 8, 128), F32), pltpu.VMEM((2, ND * 8, 128), F32),
             pltpu.VMEM((2, BINS, LAGS), BF16), pltpu.VMEM((2, BINS, LAGS), BF16), pltpu.VMEM((2, 32, LAGS), F32),
             pltpu.VMEM((144, BINS), F32), sem.REGULAR, sem.REGULAR, sem.DMA((2,)), sem.DMA((2,)), sem.DMA((2,)),

time: 77 us -> 73.3 us (0.952)
  Pallas kernels: 75.4 us -> 71.7 us
    pallas_call x1, Pallas kernels: 75.4 us -> 71.7 us  [correlate(): pl.pallas_call(correlate_kernel, out_shape=pltpu.VMEM((16, 9 * LAGS), F32...]
where the time goes in v5:
time: 73.3 us; the launch traced here: 73.2 us
  Pallas kernels  71.7 us (98%)
  local copies, waits for them, and re-layouts  0.82 us (1%)
    pallas_call x1, Pallas kernels, correlate(): pl.pallas_call(correlate_kernel, out_shape=pltpu.VMEM((16, 9 * LAGS), F32...  71.7 us

profile of v5, /device:TPU:1, one launch (start us, length us, event | category | flops | bytes accessed | tf_op | source)
XLA Modules:
  0.0 73.2 jit_solution(7077758094700449665)
XLA Ops:
  0.7 71.7 %correlate.1 = f32[16,9216]{1,0:T(8,128)S(1)} custom-call(f32[8,6,16,512]{3,2,1,0:T(8,128)} %spec_hbm.1, s32[2,64]{1,0:T(2,128)} %bitcast.6, s32[2,64]{1,0:T(2,128)} %bitcast.7, s32[1]{0:T(128)S(6)} %copy.7.count_ref), custom_call_target="tpu_custom_call" | custom-call | tf_op jit(solution)/shard_map/correlate/pallas_call | solution.py:398
  72.3 0.8 %copy.6 = f32[16,9216]{1,0:T(8,128)} copy(f32[16,9216]{1,0:T(8,128)S(1)} %correlate.1) | data formatting | bytes 1179648
